TPU v7x, 32 devices: a whole 2x2x4 slice. The times are simulated.
32 devices in a mesh: ra: 4 (over z), dec: 8 (over y, x, core).
Axes of the slice: x: 2, y: 2, z: 4, core: 2. Of those that a mesh axis runs over, the one named last changes fastest.
Arguments:
- forests: bfloat16 [8, 32, 128, 1024], P('ra', 'dec'), may hold values from -6 to 6
- resolution: float32 [8, 32, 128], P('ra', 'dec'), may hold values from 0.3 to 1.2
- pixel_range: int32 [8, 32, 2, 128], P('ra', 'dec'), may hold values from 0 to 1024, as said below
- block_pairs: int32 [4, 8, 40, 3], P('ra', 'dec'), may hold values from -1 to 7, as said below
- block_count: int32 [4, 8], P('ra', 'dec'), may hold values from 10 to 40, as said below
- separation_bin: int32 [4, 8, 40, 128, 128], P('ra', 'dec'), may hold values from 0 to 8
Outputs:
- tile_power: float32 [4, 8, 8, 128], P('ra', 'dec')
- sky_power: float32 [8, 128], replicated
Inputs may be any that keep to these rules, and one draw needn't show every extreme that they name: `pixel_range`: lo < hi for every forest; at least 256 valid pixels. `block_pairs`: each device's list names every one of its own cells once with each of the five offsets (0, 0), (0, 1), (1, -1), (1, 0), (1, 1), in an order drawn from the seed. Slots at or past block_count are ignored. `block_count`: some device has all 40 slots live in every draw.
All inputs are finite; a program needn't handle non-finite values.
Results may differ from a plain program's by a relative error of at most 0.0037.
Values may be sent and summed in bfloat16 or wider, within the bound.
No kernel may reach another device: no remote copies, remote signals or barrier semaphores. Data moves between devices by JAX's collectives and lax.ppermute only.
A program may use at most 64 MiB of HBM per device.

v0:
```python
import jax
import jax.numpy as jnp
from jax import lax
from jax.sharding import PartitionSpec as P

NSEP = 8
NKB = 128


def extended(block, sides, width):
    for axis, dim in sides:
        count = lax.axis_size(axis)
        forward = [(i, i + 1) for i in range(count - 1)]
        backward = [(target, source) for source, target in forward]
        low = lax.ppermute(
            lax.slice_in_dim(block, block.shape[dim] - width, None, axis=dim), axis, forward
        )
        high = lax.ppermute(lax.slice_in_dim(block, 0, width, axis=dim), axis, backward)
        block = jnp.concatenate([low, block, high], axis=dim)
    return block


def from_behind(value, axis, steps):
    count = lax.axis_size(axis)
    leading, last = (max(0, -steps), min(count, count - steps))
    return lax.ppermute(value, axis, [(source, source + steps) for source in range(leading, last)])


def dft_table(length, n_modes):
    sample = jnp.arange(length, dtype=jnp.int32)[:, None]
    mode_index = jnp.arange(n_modes, dtype=jnp.int32)[None, :]
    angles = (sample * mode_index % length).astype(jnp.float32) * (2.0 * jnp.pi / length)
    return jnp.concatenate([jnp.cos(angles), jnp.sin(angles)], axis=1).astype(jnp.bfloat16)


def kbin_table(n_modes, n_bins):
    column = jnp.arange(2 * n_modes, dtype=jnp.int32) % n_modes
    which = column // (n_modes // n_bins)
    return (which[:, None] == jnp.arange(n_bins, dtype=jnp.int32)[None, :]).astype(jnp.float32)


def mask_pixels(flux, pixel_range):
    position = jnp.arange(flux.shape[-1], dtype=jnp.int32)
    lower = pixel_range[..., 0, :][..., None]
    upper = pixel_range[..., 1, :][..., None]
    inside = (position >= lower) & (position < upper)
    return jnp.where(inside, flux, jnp.zeros_like(flux))


def to_spectra(masked, widths, basis):
    length = basis.shape[0]
    n_modes = basis.shape[1] // 2
    raw = jnp.dot(masked, basis, preferred_element_type=jnp.float32)
    wavenum = jnp.arange(n_modes, dtype=jnp.float32) * (2.0 * jnp.pi / length)
    wavenum = jnp.concatenate([wavenum, wavenum])
    window = jnp.exp(-0.5 * (wavenum * widths[..., None]) ** 2)
    return (raw * window).astype(jnp.bfloat16)


def block_term(grid_flat, index_a, index_b, sep_bins):
    n_sep = NSEP
    per_cell = sep_bins.shape[0]
    left = lax.dynamic_index_in_dim(grid_flat, index_a, 0, keepdims=False)
    right = lax.dynamic_index_in_dim(grid_flat, index_b, 0, keepdims=False)
    onehot = (sep_bins[None, :, :] == jnp.arange(n_sep, dtype=jnp.int32)[:, None, None]).astype(
        jnp.bfloat16
    )
    mixed = jnp.dot(
        onehot.reshape(n_sep * per_cell, per_cell), right, preferred_element_type=jnp.float32
    )
    mixed = mixed.reshape(n_sep, per_cell, -1)
    block_sum = jnp.sum(mixed * left.astype(jnp.float32)[None], axis=1)
    pair_counts = jnp.sum(onehot.reshape(n_sep, -1).astype(jnp.float32), axis=1)
    return (block_sum, pair_counts)


def per_device(forests, resolution, pixel_range, block_pairs, block_count, separation_bin):
    cells_ra, cells_dec, per_cell, length = forests.shape
    basis = dft_table(length, length // 2)
    masked = mask_pixels(forests, pixel_range)
    own_spectra = to_spectra(masked, resolution, basis)
    sided = extended(own_spectra, (("dec", 1),), 1)
    above = from_behind(sided[0:1], "ra", -1)
    padded = jnp.concatenate([sided, above], axis=0)
    cols_pad = cells_dec + 2
    grid_flat = padded.reshape(-1, per_cell, length)
    entries = block_pairs[0, 0]
    sep_bins = separation_bin[0, 0]
    live_count = block_count[0, 0]

    def slot_term(slot_index):
        entry_row = entries[slot_index]
        row_a = entry_row[0] // cells_dec
        col_a = entry_row[0] % cells_dec + 1
        index_a = row_a * cols_pad + col_a
        index_b = (row_a + entry_row[1]) * cols_pad + col_a + entry_row[2]
        return block_term(grid_flat, index_a, index_b, sep_bins[slot_index])

    start_value = (jnp.zeros((NSEP, length), jnp.float32), jnp.zeros((NSEP,), jnp.float32))

    def add_live(slot_index, carry):
        block_sum, counts = slot_term(slot_index)
        return (carry[0] + block_sum, carry[1] + counts)

    sums, counts = lax.fori_loop(0, live_count, add_live, start_value)
    binned = jnp.dot(sums, kbin_table(length // 2, NKB), precision=lax.Precision.HIGHEST)
    tile_power = (binned / (per_cell * length)).reshape(1, 1, NSEP, NKB)
    summed, all_counts = lax.psum((binned, counts), ("ra", "dec"))
    sky_power = summed / jnp.maximum(all_counts, 1.0)[:, None]
    return (tile_power, sky_power)


def solution(mesh):
    in_specs = (
        P("ra", "dec", None, None),
        P("ra", "dec", None),
        P("ra", "dec", None, None),
        P("ra", "dec", None, None),
        P("ra", "dec"),
        P("ra", "dec", None, None, None),
    )
    out_specs = (P("ra", "dec", None, None), P())
    return jax.shard_map(
        per_device, mesh=mesh, in_specs=in_specs, out_specs=out_specs, check_vma=False
    )
```

profile of v0, /device:TPU:0, one launch (start us, length us, event | category | flops | bytes accessed | tf_op | source)
XLA Modules:
  0.0 456.6 jit_solution(12260927048021557537)
XLA Ops:
  0.7 8.5 %sine_convert_fusion = (bf16[1024,512]{1,0:T(8,128)(2,1)S(1)}, bf16[1024,512]{1,0:T(8,128)(2,1)S(1)}) fusion(), kind=kLoop, calls=%fused_computation.29 | loop fusion | flops 8388608 | bytes 2097152 | tf_op jit(solution)/shard_map/convert.2
  9.2 2.9 multiply_convert_fusion
  12.2 2.4 collective-permute-start
  16.1 4.4 collective-permute-done.1
  23.2 28.7 %collective-permute-done.2 = bf16[1,6,128,1024]{3,2,1,0:T(8,128)(2,1)} collective-permute-done((bf16[1,6,128,1024]{3,2,1,0:T(8,128)(2,1)}, bf16[1,6,128,1024]{3,2,1,0:T(8,128)(2,1)}, u32[]{:S(2)}, u32[]{:S(2)}) %collective-permute-start.2) | collective-permute-done | bytes 1572896 | tf_op jit(solution)/shard_map/ppermute | solution.py:26
  51.8 3.6 pad_maximum_fusion
  55.4 343.0 %while.14 = (s32[]{:T(128)}, f32[8,1024]{1,0:T(8,128)S(1)}, f32[8]{0:T(128)S(1)}, s32[]{:T(128)}, s32[40,128,128]{2,1,0:T(8,128)}, /*index=5*/s32[40,3]{0,1:T(4,...) while((s32[]{:T(128)}, f32[8,1024]{1,0:T(8,128)S(1)}, ...), condition=%wide.region_3.4_spmd, body=%wide.region_0.3_spmd.sunk | while | flops 271319072 | bytes 2032330 | solution.py:105
  89.5 1.7 multiply_reduce_fusion.2
  98.5 1.7 multiply_reduce_fusion.2
  107.5 1.7 multiply_reduce_fusion.2
  143.5 1.7 multiply_reduce_fusion.2
  161.5 1.7 multiply_reduce_fusion.2
  170.6 1.7 multiply_reduce_fusion.2
  179.6 1.7 multiply_reduce_fusion.2
  215.6 1.7 multiply_reduce_fusion.2
  233.6 1.7 multiply_reduce_fusion.2
  242.6 1.7 multiply_reduce_fusion.2
  251.6 1.7 multiply_reduce_fusion.2
  287.7 1.7 multiply_reduce_fusion.2
  305.7 1.7 multiply_reduce_fusion.2
  314.7 1.7 multiply_reduce_fusion.2
  323.7 1.7 multiply_reduce_fusion.2
  359.8 1.7 multiply_reduce_fusion.2
  399.4 56.5 %all-reduce = (f32[8,128]{1,0:T(8,128)S(1)}, f32[8]{0:T(128)S(1)}) all-reduce(f32[8,128]{1,0:T(8,128)S(1)} %fusion.21, f32[8]{0:T(128)S(1)} %get-tuple-element.99), channel_id=1, replica_groups=mesh['ra'=4,'dec'=8] {'ra','dec'}, use_global_device_ids=true, to_apply=%region_4.5 | all-reduce | flops 1032 | bytes 8256 | tf_op jit(solution)/shard_map/psum | solution.py:108
  (312 shorter events, 148.2 us)
Async XLA Ops:
  0.6 8.5 %copy-start = (s32[2,4,2,128]{3,2,1,0:T(2,128)S(1)}, s32[2,4,2,128]{3,2,1,0:T(2,128)}, u32[]{:S(2)}) copy-start(s32[2,4,2,128]{3,2,1,0:T(2,128)} %param.10) | copy-start | bytes 24580
  0.6 8.6 %copy-start.2 = (bf16[2,4,128,1024]{3,2,1,0:T(8,128)(2,1)S(1)}, bf16[2,4,128,1024]{3,2,1,0:T(8,128)(2,1)}, u32[]{:S(2)}) copy-start(bf16[2,4,128,1024]{3,2,1,0:T(8,128)(2,1)} %param.8) | copy-start | bytes 6291460
  0.6 8.6 %copy-start.3 = (f32[2,4,128]{2,1,0:T(4,128)S(1)}, f32[2,4,128]{2,1,0:T(4,128)}, u32[]{:S(2)}) copy-start(f32[2,4,128]{2,1,0:T(4,128)} %param.9) | copy-start | bytes 12292
  12.2 3.9 collective-permute-start
  14.6 8.5 %copy-start.1 = (s32[1,1,40,3]{2,1,3,0:T(1,128)S(1)}, s32[1,1,40,3]{2,1,3,0:T(1,128)}, u32[]{:S(2)}) copy-start(s32[1,1,40,3]{2,1,3,0:T(1,128)} %param.11) | copy-start | bytes 1444
  14.6 5.9 %collective-permute-start.1 = (bf16[2,1,128,1024]{3,2,1,0:T(8,128)(2,1)S(1)}, bf16[2,1,128,1024]{3,2,1,0:T(8,128)(2,1)S(1)}, u32[]{:S(2)}, u32[]{:S(2)}) collective-permute-start(bf16[2,1,128,1024]{3,2,1,0:T(8,128)(2,1)S(1)} %get-tuple-element.122), channel_id=1, source_target_pairs={{1,0},{2,1},{3,2},{4,3},{5,4},{6,5},{7,6},{9,8},{10,9},{11,10},{12... | collective-permute-start | bytes 1572872 | tf_op jit(solution)/shard_map/ppermute | solution.py:18
  21.8 30.0 %collective-permute-start.2 = (bf16[1,6,128,1024]{3,2,1,0:T(8,128)(2,1)}, bf16[1,6,128,1024]{3,2,1,0:T(8,128)(2,1)}, u32[]{:S(2)}, u32[]{:S(2)}) collective-permute-start(bf16[1,6,128,1024]{3,2,1,0:T(8,128)(2,1)} %pad_maximum_fusion.1), channel_id=1, source_target_pairs={{8,0},{16,8},{24,16},{9,1},{17,9},{25,17},{10,2},{18,10},{26,18},{... | collective-permute-start | bytes 4718600 | tf_op jit(solution)/shard_map/ppermute | solution.py:26
where the time goes:
time: 464 us; the launch traced here: 457 us
  loops' own time  174 us (38%)
  matrix products  66.7 us (14%)
  other arithmetic  62.7 us (14%)
  local copies, waits for them, and re-layouts  57.8 us (12%)
  blocking collectives  56.5 us (12%)
  waiting for transfers between devices  33.2 us (7%)
  starting transfers between devices  5 us (1%)
    another operation x1, loops' own time, per_device(): sums, counts = lax.fori_loop(0, live_count, add_live, start_value)  174 us
    dot_general x38, matrix products, block_term(): jnp.dot(onehot.reshape(n_sep * per_cell, per_cell), right, preferred_elem...  63.4 us
    psum x1, blocking collectives, per_device(): summed, all_counts = lax.psum((binned, counts), ('ra', 'dec'))  56.5 us
    mul x38, other arithmetic, block_term(): block_sum = jnp.sum(mixed * left.astype(jnp.float32)[None], axis=1)  37.8 us
    eq x38, local copies, waits for them, and re-layouts, block_term(): sep_bins[None, :, :] == jnp.arange(n_sep, dtype=jnp.int32)[:, None, None]  32.5 us
    ppermute x1, waiting for transfers between devices, from_behind(): lax.ppermute(value, axis, [(source, source + steps) for source in range(l...  28.7 us
    slice x38, local copies, waits for them, and re-layouts, slot_term(): index_b = (row_a + entry_row[1]) * cols_pad + col_a + entry_row[2]  22.3 us
    reduce_sum x38, other arithmetic, block_term(): pair_counts = jnp.sum(onehot.reshape(n_sep, -1).astype(jnp.float32), axis=1)  9.44 us
  transfers between devices with their start and end apart: 3, of which 3 were waited for; matrix products, arithmetic and copies ran while one was open for 0% of the time, Pallas kernels for 0%

commit v1 on v0

--- a/solution.py
+++ b/solution.py
@@ -105,7 +105,7 @@
     sums, counts = lax.fori_loop(0, live_count, add_live, start_value)
     binned = jnp.dot(sums, kbin_table(length // 2, NKB), precision=lax.Precision.HIGHEST)
     tile_power = (binned / (per_cell * length)).reshape(1, 1, NSEP, NKB)
-    summed, all_counts = lax.psum((binned, counts), ("ra", "dec"))
+    summed, all_counts = lax.psum(lax.psum((binned, counts), "dec"), "ra")
     sky_power = summed / jnp.maximum(all_counts, 1.0)[:, None]
     return (tile_power, sky_power)
 

time: 464 us -> 446 us (0.961)
  blocking collectives: 56.5 us -> 40.7 us
    psum x1 -> x2, blocking collectives: 56.5 us -> 40.7 us  [per_device(): summed, all_counts = lax.psum(lax.psum((binned, counts), 'dec'), 'ra')]
where the time goes in v1:
time: 446 us; the launch traced here: 439 us
  loops' own time  172 us (39%)
  matrix products  66.6 us (15%)
  other arithmetic  62.7 us (14%)
  local copies, waits for them, and re-layouts  57.1 us (13%)
  blocking collectives  40.7 us (9%)
  waiting for transfers between devices  33.2 us (7%)
  starting transfers between devices  5 us (1%)
    another operation x1, loops' own time, per_device(): sums, counts = lax.fori_loop(0, live_count, add_live, start_value)  172 us
    dot_general x38, matrix products, block_term(): jnp.dot(onehot.reshape(n_sep * per_cell, per_cell), right, preferred_elem...  63.4 us
    psum x2, blocking collectives, per_device(): summed, all_counts = lax.psum(lax.psum((binned, counts), 'dec'), 'ra')  40.7 us
    mul x38, other arithmetic, block_term(): block_sum = jnp.sum(mixed * left.astype(jnp.float32)[None], axis=1)  37.8 us
    eq x38, local copies, waits for them, and re-layouts, block_term(): sep_bins[None, :, :] == jnp.arange(n_sep, dtype=jnp.int32)[:, None, None]  32.5 us
    ppermute x1, waiting for transfers between devices, from_behind(): lax.ppermute(value, axis, [(source, source + steps) for source in range(l...  28.7 us
    slice x38, local copies, waits for them, and re-layouts, slot_term(): index_b = (row_a + entry_row[1]) * cols_pad + col_a + entry_row[2]  21.6 us
    reduce_sum x38, other arithmetic, block_term(): pair_counts = jnp.sum(onehot.reshape(n_sep, -1).astype(jnp.float32), axis=1)  9.44 us
  transfers between devices with their start and end apart: 3, of which 3 were waited for; matrix products, arithmetic and copies ran while one was open for 0% of the time, Pallas kernels for 0%

profile of v1, /device:TPU:0, one launch (start us, length us, event | category | flops | bytes accessed | tf_op | source)
XLA Modules:
  0.0 438.7 jit_solution(1928310419859316378)
XLA Ops:
  0.7 8.5 %sine_convert_fusion = (bf16[1024,512]{1,0:T(8,128)(2,1)S(1)}, bf16[1024,512]{1,0:T(8,128)(2,1)S(1)}) fusion(), kind=kLoop, calls=%fused_computation.29 | loop fusion | flops 8388608 | bytes 2097152 | tf_op jit(solution)/shard_map/convert.2
  9.2 2.9 multiply_convert_fusion
  12.2 2.4 collective-permute-start
  16.1 4.4 %collective-permute-done.1 = bf16[2,1,128,1024]{3,2,1,0:T(8,128)(2,1)S(1)} collective-permute-done((bf16[2,1,128,1024]{3,2,1,0:T(8,128)(2,1)S(1)}, bf16[2,1,128,1024]{3,2,1,0:T(8,128)(2,1)S(1)}, u32[]{:S(2)}, u32[]{:S(2)}) %collective-permute-start.1) | collective-permute-done | bytes 524320 | tf_op jit(solution)/shard_map/ppermute | solution.py:18
  23.2 28.7 %collective-permute-done.2 = bf16[1,6,128,1024]{3,2,1,0:T(8,128)(2,1)} collective-permute-done((bf16[1,6,128,1024]{3,2,1,0:T(8,128)(2,1)}, bf16[1,6,128,1024]{3,2,1,0:T(8,128)(2,1)}, u32[]{:S(2)}, u32[]{:S(2)}) %collective-permute-start.2) | collective-permute-done | bytes 1572896 | tf_op jit(solution)/shard_map/ppermute | solution.py:26
  51.8 3.6 pad_maximum_fusion
  55.4 340.8 %while.14 = (s32[]{:T(128)}, f32[8,1024]{1,0:T(8,128)S(1)}, f32[8]{0:T(128)S(1)}, s32[]{:T(128)}, s32[40,128,128]{2,1,0:T(8,128)}, /*index=5*/s32[40,3]{0,1:T(4,...) while((s32[]{:T(128)}, f32[8,1024]{1,0:T(8,128)S(1)}, ...), condition=%wide.region_3.4_spmd, body=%wide.region_0.3_spmd.sunk | while | flops 271319072 | bytes 2032330 | solution.py:105
  62.4 1.7 multiply_reduce_fusion.2
  71.4 1.7 multiply_reduce_fusion.2
  80.3 1.7 multiply_reduce_fusion.2
  89.3 1.7 multiply_reduce_fusion.2
  98.2 1.7 multiply_reduce_fusion.2
  107.2 1.7 multiply_reduce_fusion.2
  116.1 1.7 multiply_reduce_fusion.2
  125.1 1.7 multiply_reduce_fusion.2
  134.0 1.7 multiply_reduce_fusion.2
  143.0 1.7 multiply_reduce_fusion.2
  151.9 1.7 multiply_reduce_fusion.2
  160.9 1.7 multiply_reduce_fusion.2
  169.8 1.7 multiply_reduce_fusion.2
  178.8 1.7 multiply_reduce_fusion.2
  250.4 1.7 multiply_reduce_fusion.2
  397.2 12.1 %all-reduce = (f32[8,128]{1,0:T(8,128)S(1)}, f32[8]{0:T(128)S(1)}) all-reduce(f32[8,128]{1,0:T(8,128)S(1)} %fusion.21, f32[8]{0:T(128)S(1)} %get-tuple-element.99), channel_id=1, replica_groups=mesh['ra'=4,'dec'=8] {'dec'}, use_global_device_ids=true, to_apply=%region_4.5 | all-reduce | flops 1032 | bytes 8256 | tf_op jit(solution)/shard_map/psum | solution.py:108
  409.3 28.6 %all-reduce.1 = (f32[8,128]{1,0:T(8,128)S(1)}, f32[8]{0:T(128)S(1)}) all-reduce(f32[8,128]{1,0:T(8,128)S(1)} %get-tuple-element.114, f32[8]{0:T(128)S(1)} %get-tuple-element.115), channel_id=1, replica_groups=mesh['ra'=4,'dec'=8] {'ra'}, use_global_device_ids=true, to_apply=%region_5.6 | all-reduce | flops 1032 | bytes 8256 | tf_op jit(solution)/shard_map/psum | solution.py:108
  (313 shorter events, 149.2 us)
Async XLA Ops:
  0.6 8.5 %copy-start = (s32[2,4,2,128]{3,2,1,0:T(2,128)S(1)}, s32[2,4,2,128]{3,2,1,0:T(2,128)}, u32[]{:S(2)}) copy-start(s32[2,4,2,128]{3,2,1,0:T(2,128)} %param.10) | copy-start | bytes 24580
  0.6 8.6 %copy-start.2 = (bf16[2,4,128,1024]{3,2,1,0:T(8,128)(2,1)S(1)}, bf16[2,4,128,1024]{3,2,1,0:T(8,128)(2,1)}, u32[]{:S(2)}) copy-start(bf16[2,4,128,1024]{3,2,1,0:T(8,128)(2,1)} %param.8) | copy-start | bytes 6291460
  0.6 8.6 %copy-start.3 = (f32[2,4,128]{2,1,0:T(4,128)S(1)}, f32[2,4,128]{2,1,0:T(4,128)}, u32[]{:S(2)}) copy-start(f32[2,4,128]{2,1,0:T(4,128)} %param.9) | copy-start | bytes 12292
  12.2 3.9 collective-permute-start
  14.6 8.5 %copy-start.1 = (s32[1,1,40,3]{2,1,3,0:T(1,128)S(1)}, s32[1,1,40,3]{2,1,3,0:T(1,128)}, u32[]{:S(2)}) copy-start(s32[1,1,40,3]{2,1,3,0:T(1,128)} %param.11) | copy-start | bytes 1444
  14.6 5.9 %collective-permute-start.1 = (bf16[2,1,128,1024]{3,2,1,0:T(8,128)(2,1)S(1)}, bf16[2,1,128,1024]{3,2,1,0:T(8,128)(2,1)S(1)}, u32[]{:S(2)}, u32[]{:S(2)}) collective-permute-start(bf16[2,1,128,1024]{3,2,1,0:T(8,128)(2,1)S(1)} %get-tuple-element.124), channel_id=1, source_target_pairs={{1,0},{2,1},{3,2},{4,3},{5,4},{6,5},{7,6},{9,8},{10,9},{11,10},{12... | collective-permute-start | bytes 1572872 | tf_op jit(solution)/shard_map/ppermute | solution.py:18
  21.9 30.0 %collective-permute-start.2 = (bf16[1,6,128,1024]{3,2,1,0:T(8,128)(2,1)}, bf16[1,6,128,1024]{3,2,1,0:T(8,128)(2,1)}, u32[]{:S(2)}, u32[]{:S(2)}) collective-permute-start(bf16[1,6,128,1024]{3,2,1,0:T(8,128)(2,1)} %pad_maximum_fusion.1), channel_id=1, source_target_pairs={{8,0},{16,8},{24,16},{9,1},{17,9},{25,17},{10,2},{18,10},{26,18},{... | collective-permute-start | bytes 4718600 | tf_op jit(solution)/shard_map/ppermute | solution.py:26
